TPU v7x, 32 devices: a whole 2x2x4 slice. The times are simulated.
32 devices in a mesh: rows: 16 (over z, y, x), cols: 2 (over core).
Axes of the slice: x: 2, y: 2, z: 4, core: 2. Of those that a mesh axis runs over, the one named last changes fastest.
Arguments:
- snapshots: bfloat16 [16384, 2, 2, 128], P('rows', 'cols'), may hold values from -12 to 12
- scales: float32 [32, 2, 2], P('rows'), may hold values from 0.2 to 9
Outputs:
- coefficients: float32 [128, 2, 2, 128], P(None, 'cols')
- updated: bfloat16 [16384, 2, 2, 128], P('rows', 'cols')
All inputs are finite; a program needn't handle non-finite values.
Results may differ from a plain program's by a relative error of at most 0.012.
Values may be sent and summed in bfloat16 or wider, within the bound.
No kernel may reach another device: no remote copies, remote signals or barrier semaphores. Data moves between devices by JAX's collectives and lax.ppermute only.
A program may use at most 64 MiB of HBM per device.

v0:
```python
import math
import jax
import jax.numpy as jnp
from jax import lax
from jax.sharding import PartitionSpec as P

HIGH = lax.Precision.HIGHEST


def spread(shard, axis, root):
    mine = lax.axis_index(axis) == root
    return lax.psum(jnp.where(mine, shard, jnp.zeros_like(shard)), axis)


def product(left, right):
    return jnp.dot(left, right, precision=HIGH, preferred_element_type=jnp.float32)


def scaled_values(snapshots, scales, group):
    points, _, rounds, width = snapshots.shape
    nblock = scales.shape[0]
    own_scales = lax.dynamic_slice_in_dim(scales, group, 1, 1)[:, 0, :]
    shaped = snapshots.astype(jnp.float32).reshape(nblock, points // nblock, rounds, width)
    return (shaped * own_scales[:, None, :, None]).reshape(points, rounds * width)


def upper_inverse(gram):
    width = gram.shape[0]
    positions = jnp.arange(width, dtype=jnp.int32)

    def factor_step(column_index, state_pair):
        remaining, lower_factor = state_pair
        picker = (positions == column_index).astype(jnp.float32)
        column = jnp.sum(remaining * picker[None, :], axis=1)
        pivot_value = jnp.sum(column * picker)
        column = jnp.where(positions >= column_index, column / jnp.sqrt(pivot_value), 0.0)
        lower_factor = lower_factor + column[:, None] * picker[None, :]
        remaining = remaining - column[:, None] * column[None, :]
        return (remaining, lower_factor)

    start_lower = jnp.zeros((width, width), jnp.float32)
    _, lower_factor = lax.fori_loop(0, width, factor_step, (gram, start_lower))

    def solve_step(row_index, inverse_rows):
        picker = (positions == row_index).astype(jnp.float32)
        lower_row = jnp.sum(lower_factor * picker[:, None], axis=0)
        diagonal_entry = jnp.sum(lower_row * picker)
        earlier = jnp.where(positions < row_index, lower_row, 0.0)
        new_row = (picker - product(earlier[None, :], inverse_rows)[0]) / diagonal_entry
        return inverse_rows + picker[:, None] * new_row[None, :]

    lower_inverse = lax.fori_loop(0, width, solve_step, jnp.zeros((width, width), jnp.float32))
    return lower_inverse.T


def shards(snapshots, scales):
    points, _, rounds, width = snapshots.shape
    group = lax.axis_index("cols")
    values = scaled_values(snapshots, scales, group)
    panel = values[:, :width]
    gram = lax.psum(product(panel.T, panel), "rows")
    inverse = upper_inverse(gram)
    basis = spread(product(panel, inverse).astype(jnp.bfloat16), "cols", 0).astype(jnp.float32)
    raw = lax.psum(product(basis.T, values), "rows")
    root = math.sqrt(points * lax.axis_size("rows"))
    remainder = values - product(basis, raw)
    leading = jnp.where(group == 0, root * basis, remainder[:, :width])
    whole = jnp.concatenate([leading, remainder[:, width:]], axis=1)
    updated = whole.astype(jnp.bfloat16).reshape(points, 1, rounds, width)
    coefficients = (raw / root).reshape(width, 1, rounds, width)
    return (coefficients, updated)


def solution(mesh):
    return jax.shard_map(
        shards,
        mesh=mesh,
        in_specs=(P("rows", "cols", None, None), P("rows", None, None)),
        out_specs=(P(None, "cols", None, None), P("rows", "cols", None, None)),
        check_vma=False,
    )
```

profile of v0, /device:TPU:0, one launch (start us, length us, event | category | flops | bytes accessed | tf_op | source)
XLA Modules:
  0.0 862.3 jit_solution(12025838508278605038)
XLA Ops:
  7.2 1.1 bitcast_convert_fusion
  8.9 1.7 fusion.19
  10.6 108.1 %all-reduce.4.cloned.1.call-done = f32[128,128]{1,0:T(8,128)} async-done(((f32[128,128]{1,0:T(8,128)}), f32[128,128]{1,0:T(8,128)}) %all-reduce.4.cloned.1.call-update) | async-done | bytes 65552 | tf_op jit(solution)/shard_map/psum | solution.py:61
  118.8 393.0 %while.32 = (s32[]{:T(128)}, f32[128,128]{1,0:T(8,128)}, f32[128,128]{1,0:T(8,128)S(1)}, s32[]{:T(128)}, s32[]{:T(128)}) while((s32[]{:T(128)}, f32[128,128]{1,0:T(8,128)}, f32[128,128]{1,0:T(8,128)S(1)}, s32[]{:T(128)}, s32[]{:T(128)}) %tuple.74), condition=%wide.region_4.5_spmd.clone.clone, body=%wide.region_1.4_spmd.clone.clone.sunk | while | flops 115586 | bytes 856219 | solution.py:42
  118.8 1.0 multiply_reduce_fusion.4
  121.8 1.0 multiply_reduce_fusion.4
  124.9 1.0 multiply_reduce_fusion.4
  128.0 1.0 multiply_reduce_fusion.4
  131.1 1.0 multiply_reduce_fusion.4
  134.1 1.0 multiply_reduce_fusion.4
  137.2 1.0 multiply_reduce_fusion.4
  140.3 1.0 multiply_reduce_fusion.4
  143.3 1.0 multiply_reduce_fusion.4
  146.4 1.0 multiply_reduce_fusion.4
  149.5 1.0 multiply_reduce_fusion.4
  152.5 1.0 multiply_reduce_fusion.4
  155.6 1.0 multiply_reduce_fusion.4
  158.7 1.0 multiply_reduce_fusion.4
  511.7 210.5 %while.33 = (s32[]{:T(128)}, f32[128,128]{1,0:T(8,128)S(1)}, f32[128,128]{1,0:T(8,128)S(1)}, s32[]{:T(128)}, s32[]{:T(128)}) while((s32[]{:T(128)}, f32[128,128]{1,0:T(8,128)S(1)}, f32[128,128]{1,0:T(8,128)S(1)}, s32[]{:T(128)}, s32[]{:T(128)}) %tuple.77), condition=%wide.region_8.9_spmd.clone.clone, body=%wide.region_5.8_spmd.clone.clone.sunk | while | flops 296194 | bytes 266332 | solution.py:52
  722.2 1.3 fusion.16
  723.6 17.4 %all-reduce.6.cloned.1.call-done = bf16[1024,128]{1,0:T(8,128)(2,1)} async-done(((bf16[1024,128]{1,0:T(8,128)(2,1)}), bf16[1024,128]{1,0:T(8,128)(2,1)}) %all-reduce.6.cloned.1.call-update) | async-done | bytes 262160 | tf_op jit(solution)/shard_map/psum | solution.py:12
  741.0 2.3 fusion.21
  743.3 109.1 %all-reduce.8.cloned.1.call-done = f32[128,256]{1,0:T(8,128)} async-done(((f32[128,256]{1,0:T(8,128)}), f32[128,256]{1,0:T(8,128)}) %all-reduce.8.cloned.1.call-update) | async-done | bytes 131088 | tf_op jit(solution)/shard_map/psum | solution.py:64
  852.4 1.5 convolution_subtract_fusion
  (1800 shorter events, 493.1 us)
Async XLA Ops:
  7.2 111.6 %all-reduce.4.cloned.1.call-start = ((), (), s32[]{:S(2)}) async-start(), calls=%async_computation | async-start | bytes 131072 | tf_op jit(solution)/shard_map/psum | solution.py:61
  10.6 730.5 %all-reduce.6.cloned.1.call-start = ((), (), s32[]{:S(2)}) async-start(), calls=%async_computation.1 | async-start | bytes 524288 | tf_op jit(solution)/shard_map/psum | solution.py:12
  118.8 2.3 copy-start.1
  121.8 2.3 copy-start.1
  124.9 2.3 copy-start.1
  128.0 2.3 copy-start.1
  131.1 2.3 copy-start.1
  134.1 2.3 copy-start.1
  137.2 2.3 copy-start.1
  140.3 2.3 copy-start.1
  143.3 2.3 copy-start.1
  146.4 2.3 copy-start.1
  149.5 2.3 copy-start.1
  152.5 2.3 copy-start.1
  155.6 2.3 copy-start.1
  158.7 2.3 copy-start.1
  161.8 2.3 copy-start.1
  164.8 2.3 copy-start.1
  167.9 2.3 copy-start.1
  171.0 2.3 copy-start.1
  174.0 2.3 copy-start.1
  177.1 2.3 copy-start.1
  723.6 128.9 %all-reduce.8.cloned.1.call-start = ((), (), s32[]{:S(2)}) async-start(), calls=%async_computation.2 | async-start | bytes 262144 | tf_op jit(solution)/shard_map/psum | solution.py:64
  741.0 111.4 %copy-start.3 = (bf16[1024,128]{1,0:T(8,128)(2,1)S(1)}, bf16[1024,128]{1,0:T(8,128)(2,1)}, u32[]{:S(2)}) copy-start(bf16[1024,128]{1,0:T(8,128)(2,1)} %all-reduce.6.cloned.1.call-done) | copy-start | bytes 786436
  (238 other events, 334.5 us)
Sparse Core Ops, SparseCore 0:
  14.1 104.6 all-reduce.3
  723.7 17.3 all-reduce.5
  747.1 105.3 all-reduce.7
where the time goes:
time: 871 us; the launch traced here: 862 us
  other arithmetic  326 us (37%)
  waiting for transfers between devices  235 us (27%)
  matrix products  109 us (13%)
  loops' own time  98.7 us (11%)
  local copies, waits for them, and re-layouts  80.3 us (9%)
  between operations  13.9 us (2%)
    reduce_sum x128, other arithmetic, factor_step(): column = jnp.sum(remaining * picker[None, :], axis=1)  129 us
    psum x1, waiting for transfers between devices, shards(): raw = lax.psum(product(basis.T, values), 'rows')  109 us
    dot_general x132, matrix products, product(): jnp.dot(left, right, precision=HIGH, preferred_element_type=jnp.float32)  109 us
    psum x1, waiting for transfers between devices, shards(): gram = lax.psum(product(panel.T, panel), 'rows')  108 us
    another operation x1, loops' own time, upper_inverse(): _, lower_factor = lax.fori_loop(0, width, factor_step, (gram, start_lower))  94.7 us
    while x512, local copies, waits for them, and re-layouts  78.3 us
    reduce_sum x128, other arithmetic, factor_step(): pivot_value = jnp.sum(column * picker)  78.3 us
    reduce_sum x128, other arithmetic, solve_step(): diagonal_entry = jnp.sum(lower_row * picker)  78.1 us
  transfers between devices with their start and end apart: 3, of which 3 were waited for; matrix products, arithmetic and copies ran while one was open for 0% of the time, Pallas kernels for 0%

commit v1 on v0

--- a/solution.py
+++ b/solution.py
@@ -9,7 +9,7 @@
 
 def spread(shard, axis, root):
     mine = lax.axis_index(axis) == root
-    return lax.psum(jnp.where(mine, shard, jnp.zeros_like(shard)), axis)
+    return jnp.sum(lax.all_gather(jnp.where(mine, shard, jnp.zeros_like(shard)), axis), axis=0)
 
 
 def product(left, right):

time: 871 us -> 849 us (0.975)
  waiting for transfers between devices: 235 us -> 212 us
    psum x1 -> x0, waiting for transfers between devices: 17.4 us -> none  [spread(): return lax.psum(jnp.where(mine, shard, jnp.zeros_like(shard)), axis)]
  transfers between devices with their start and end apart: 3 -> 2, of which waited for: 3 -> 2; matrix products, arithmetic and copies ran while one was open for 0% -> 0% of each run, Pallas kernels for 0% -> 0%
where the time goes in v1:
time: 849 us; the launch traced here: 840 us
  other arithmetic  326 us (38%)
  waiting for transfers between devices  212 us (25%)
  matrix products  107 us (13%)
  loops' own time  98.7 us (12%)
  local copies, waits for them, and re-layouts  80.3 us (9%)
  between operations  14.2 us (2%)
    reduce_sum x128, other arithmetic, factor_step(): column = jnp.sum(remaining * picker[None, :], axis=1)  129 us
    psum x1, waiting for transfers between devices, shards(): gram = lax.psum(product(panel.T, panel), 'rows')  108 us
    dot_general x132, matrix products, product(): jnp.dot(left, right, precision=HIGH, preferred_element_type=jnp.float32)  107 us
    psum x1, waiting for transfers between devices, shards(): raw = lax.psum(product(basis.T, values), 'rows')  103 us
    another operation x1, loops' own time, upper_inverse(): _, lower_factor = lax.fori_loop(0, width, factor_step, (gram, start_lower))  94.7 us
    while x512, local copies, waits for them, and re-layouts  78.3 us
    reduce_sum x128, other arithmetic, factor_step(): pivot_value = jnp.sum(column * picker)  78.3 us
    reduce_sum x128, other arithmetic, solve_step(): diagonal_entry = jnp.sum(lower_row * picker)  78.1 us
  transfers between devices with their start and end apart: 2, of which 2 were waited for; matrix products, arithmetic and copies ran while one was open for 0% of the time, Pallas kernels for 0%

profile of v1, /device:TPU:0, one launch (start us, length us, event | category | flops | bytes accessed | tf_op | source)
XLA Modules:
  0.0 840.1 jit_solution(7264948017639785124)
XLA Ops:
  7.2 1.1 bitcast_convert_fusion
  8.9 1.7 fusion.19
  10.6 108.1 %all-reduce.3.cloned.1.call-done = f32[128,128]{1,0:T(8,128)} async-done(((f32[128,128]{1,0:T(8,128)}), f32[128,128]{1,0:T(8,128)}) %all-reduce.3.cloned.1.call-update) | async-done | bytes 65552 | tf_op jit(solution)/shard_map/psum | solution.py:61
  118.8 393.0 %while.32 = (s32[]{:T(128)}, f32[128,128]{1,0:T(8,128)}, f32[128,128]{1,0:T(8,128)S(1)}, s32[]{:T(128)}, s32[]{:T(128)}) while((s32[]{:T(128)}, f32[128,128]{1,0:T(8,128)}, f32[128,128]{1,0:T(8,128)S(1)}, s32[]{:T(128)}, s32[]{:T(128)}) %tuple.74), condition=%wide.region_4.5_spmd.clone.clone, body=%wide.region_1.4_spmd.clone.clone.sunk | while | flops 115586 | bytes 856219 | solution.py:42
  118.8 1.0 multiply_reduce_fusion.4
  121.8 1.0 multiply_reduce_fusion.4
  124.9 1.0 multiply_reduce_fusion.4
  128.0 1.0 multiply_reduce_fusion.4
  131.1 1.0 multiply_reduce_fusion.4
  134.1 1.0 multiply_reduce_fusion.4
  137.2 1.0 multiply_reduce_fusion.4
  140.3 1.0 multiply_reduce_fusion.4
  143.3 1.0 multiply_reduce_fusion.4
  146.4 1.0 multiply_reduce_fusion.4
  149.5 1.0 multiply_reduce_fusion.4
  152.5 1.0 multiply_reduce_fusion.4
  155.6 1.0 multiply_reduce_fusion.4
  158.7 1.0 multiply_reduce_fusion.4
  161.8 1.0 multiply_reduce_fusion.4
  511.7 210.5 %while.33 = (s32[]{:T(128)}, f32[128,128]{1,0:T(8,128)S(1)}, f32[128,128]{1,0:T(8,128)S(1)}, s32[]{:T(128)}, s32[]{:T(128)}) while((s32[]{:T(128)}, f32[128,128]{1,0:T(8,128)S(1)}, f32[128,128]{1,0:T(8,128)S(1)}, s32[]{:T(128)}, s32[]{:T(128)}) %tuple.77), condition=%wide.region_8.9_spmd.clone.clone, body=%wide.region_5.8_spmd.clone.clone.sunk | while | flops 296194 | bytes 266332 | solution.py:52
  722.8 2.2 all-gather
  725.2 1.2 fusion.21
  726.5 103.5 %all-reduce.5.cloned.1.call-done = f32[128,256]{1,0:T(8,128)} async-done(((f32[128,256]{1,0:T(8,128)}), f32[128,256]{1,0:T(8,128)}) %all-reduce.5.cloned.1.call-update) | async-done | bytes 131088 | tf_op jit(solution)/shard_map/psum | solution.py:64
  829.9 1.5 convolution_subtract_fusion
  (1797 shorter events, 492.8 us)
Async XLA Ops:
  7.2 111.6 %all-reduce.3.cloned.1.call-start = ((), (), s32[]{:S(2)}) async-start(), calls=%async_computation | async-start | bytes 131072 | tf_op jit(solution)/shard_map/psum | solution.py:61
  10.6 819.4 %all-reduce.5.cloned.1.call-start = ((), (), s32[]{:S(2)}) async-start(), calls=%async_computation.1 | async-start | bytes 262144 | tf_op jit(solution)/shard_map/psum | solution.py:64
  118.8 2.3 copy-start.1
  121.8 2.3 copy-start.1
  124.9 2.3 copy-start.1
  128.0 2.3 copy-start.1
  131.1 2.3 copy-start.1
  134.1 2.3 copy-start.1
  137.2 2.3 copy-start.1
  140.3 2.3 copy-start.1
  143.3 2.3 copy-start.1
  146.4 2.3 copy-start.1
  149.5 2.3 copy-start.1
  152.5 2.3 copy-start.1
  155.6 2.3 copy-start.1
  158.7 2.3 copy-start.1
  161.8 2.3 copy-start.1
  164.8 2.3 copy-start.1
  167.9 2.3 copy-start.1
  171.0 2.3 copy-start.1
  174.0 2.3 copy-start.1
  177.1 2.3 copy-start.1
  180.2 2.3 copy-start.1
  183.2 2.3 copy-start.1
  (236 other events, 329.8 us)
Sparse Core Ops, SparseCore 0:
  14.1 104.6 all-reduce.2
  726.6 103.2 all-reduce.4
